TPU v7x, 128 devices: a whole 4x4x4 slice. The times are simulated.
128 devices in a mesh: dp: 4 (over y), expert: 32 (over z, x, core).
Axes of the slice: x: 4, y: 4, z: 4, core: 2. Of those that a mesh axis runs over, the one named last changes fastest.
Arguments:
- stream: bfloat16 [16384, 7168], P(('dp', 'expert')), may hold values from -30 to 30
- heads_out: bfloat16 [16384, 16384], P(('dp', 'expert')), may hold values from -6 to 6
- cotangent: bfloat16 [16384, 7168], P(('dp', 'expert')), may hold values from -6 to 6
- adapter_down: bfloat16 [16, 16384], replicated, may hold values from -0.046875 to 0.046875
- adapter_raise_factor: bfloat16 [16, 7168], replicated, may hold values from -0.59765625 to 0.59765625
- norm_gain: float32 [7168], replicated, may hold values from 0.5 to 2
- router: bfloat16 [256, 7168], replicated, may hold values from -0.125 to 0.125
- expert_ids: int32 [16384, 8], P(('dp', 'expert')), may hold values from 0 to 255, as said below
- w_gate_up: bfloat16 [32, 7168, 2, 1024], P('expert', None, None, 'dp'), may hold values from -0.0625 to 0.0625
- w_down: bfloat16 [32, 1024, 7168], P('expert', 'dp'), may hold values from -0.1875 to 0.1875
Outputs:
- residual_stream_gradient: bfloat16 [16384, 7168], P(('dp', 'expert'))
- grad_down: float32 [16, 16384], replicated
- raise_factor_gradient: float32 [16, 7168], replicated
Inputs may be any that keep to these rules, and one draw needn't show every extreme that they name: `expert_ids`: each row names 8 different experts. Within each aligned block of 128 rows (the tokens of one device) every expert below 32 is named by at most 6 rows, and one of them is named by exactly 6 rows in every block; the order of a row's ids carries no meaning.
All inputs are finite; a program needn't handle non-finite values.
Results may differ from a plain program's by a relative error of at most 0.0085.
Values may be sent and summed in bfloat16 or wider, within the bound.
No kernel may reach another device: no remote copies, remote signals or barrier semaphores. Data moves between devices by JAX's collectives and lax.ppermute only.
A program may use at most 192 MiB of HBM per device.

v0:
```python
import jax
import jax.numpy as jnp
from jax import lax
from jax.sharding import PartitionSpec as P

ALL_EXP = 256
CAP = 6


adapter_scale_factor = 2.0
route_scale = 2.5
norm_eps = 1e-06


def repeat_rows(block, count):
    copies = jnp.broadcast_to(block[None], (count,) + block.shape)
    return copies.reshape((count * block.shape[0],) + block.shape[1:])


def expert_rows(rows_in, rows_grad, w_gate_up, w_down):
    quarter = w_down.shape[1]
    width = w_down.shape[2]
    flat_in = rows_in.reshape(-1, width)
    flat_grad = rows_grad.reshape(-1, width)
    joined = w_gate_up.reshape(width, 2 * quarter)
    lowered = w_down.reshape(quarter, width)
    projected = jnp.dot(flat_in, joined, preferred_element_type=jnp.float32)
    gate_pre = projected[:, :quarter]
    up_pre = projected[:, quarter:]
    sigma_gate = jax.nn.sigmoid(gate_pre)
    activated = gate_pre * sigma_gate
    hidden = (activated * up_pre).astype(jnp.bfloat16)
    hidden_grad = jnp.einsum("md,hd->mh", flat_grad, lowered, preferred_element_type=jnp.float32)
    slot_dots = jnp.sum(hidden.astype(jnp.float32) * hidden_grad, axis=1)
    pre_grad = jnp.concatenate(
        [
            hidden_grad * up_pre * sigma_gate * (1.0 + gate_pre * (1.0 - sigma_gate)),
            hidden_grad * activated,
        ],
        axis=1,
    ).astype(jnp.bfloat16)
    partial_rows = jnp.einsum("mk,dk->md", pre_grad, joined, preferred_element_type=jnp.float32)
    return (partial_rows, slot_dots)


def local(
    stream,
    heads_out,
    cotangent,
    adapter_down,
    adapter_raise_factor,
    norm_gain,
    router,
    expert_ids,
    w_gate_up,
    w_down,
):
    tokens_here = stream.shape[0]
    width = stream.shape[1]
    experts_here = lax.axis_size("expert")
    replicas = lax.axis_size("dp")
    hidden_code = jnp.einsum(
        "th,rh->tr", heads_out, adapter_down, preferred_element_type=jnp.float32
    ).astype(jnp.bfloat16)
    combined_result = stream.astype(jnp.float32) + adapter_scale_factor * jnp.dot(
        hidden_code, adapter_raise_factor, preferred_element_type=jnp.float32
    )
    inverse = lax.rsqrt(
        jnp.mean(combined_result * combined_result, axis=1, keepdims=True) + norm_eps
    )
    normed = combined_result * inverse
    normed_in = (normed * norm_gain).astype(jnp.bfloat16)
    logits = jnp.einsum("td,ed->te", normed_in, router, preferred_element_type=jnp.float32)
    affinity = jax.nn.sigmoid(logits)
    choose = expert_ids[:, :, None] == jnp.arange(ALL_EXP, dtype=jnp.int32)[None, None, :]
    chosen = jnp.sum(jnp.where(choose, affinity[:, None, :], 0.0), axis=2)
    affin_sum = jnp.sum(chosen, axis=1, keepdims=True)
    gate_weights = route_scale * chosen / affin_sum
    window_hit = expert_ids[:, :, None] == jnp.arange(experts_here, dtype=jnp.int32)[None, None, :]
    member = jnp.sum(window_hit.astype(jnp.int32), axis=1)
    gate_window = jnp.sum(jnp.where(window_hit, gate_weights[:, :, None], 0.0), axis=1)
    position = jnp.cumsum(member, axis=0) - member
    slot_hit = (member[:, :, None] == 1) & (
        position[:, :, None] == jnp.arange(CAP, dtype=jnp.int32)[None, None, :]
    )
    slot_count = experts_here * CAP
    pick = slot_hit.reshape(tokens_here, slot_count).astype(jnp.bfloat16)
    send_in = (
        jnp.einsum("ts,td->sd", pick, normed_in, preferred_element_type=jnp.float32)
        .astype(jnp.bfloat16)
        .reshape(experts_here, CAP, width)
    )
    send_grad = (
        jnp.einsum("ts,td->sd", pick, cotangent, preferred_element_type=jnp.float32)
        .astype(jnp.bfloat16)
        .reshape(experts_here, CAP, width)
    )
    rows_in, rows_grad = (
        lax.all_to_all(
            repeat_rows(send_in, replicas),
            ("dp", "expert"),
            split_axis=0,
            concat_axis=0,
            tiled=True,
        ),
        lax.all_to_all(
            repeat_rows(send_grad, replicas),
            ("dp", "expert"),
            split_axis=0,
            concat_axis=0,
            tiled=True,
        ),
    )
    partial_rows, slot_dots = expert_rows(rows_in, rows_grad, w_gate_up, w_down)
    partial_rows = partial_rows.reshape(replicas * experts_here, CAP, width)
    slot_dots = slot_dots.reshape(replicas * experts_here, CAP)
    back_rows, back_dots = (
        lax.all_to_all(
            partial_rows.astype(jnp.bfloat16),
            ("dp", "expert"),
            split_axis=0,
            concat_axis=0,
            tiled=True,
        ),
        lax.all_to_all(
            slot_dots.astype(jnp.bfloat16),
            ("dp", "expert"),
            split_axis=0,
            concat_axis=0,
            tiled=True,
        ),
    )
    returned = jnp.sum(
        back_rows.reshape(replicas, experts_here, CAP, width).astype(jnp.float32), axis=0
    ).astype(jnp.bfloat16)
    dot_sum = jnp.sum(
        back_dots.reshape(replicas, experts_here, CAP).astype(jnp.float32), axis=0
    ).astype(jnp.bfloat16)
    combine_weights = (
        jnp.where(slot_hit, gate_window[:, :, None], 0.0)
        .reshape(tokens_here, slot_count)
        .astype(jnp.bfloat16)
    )
    unit_grad = jnp.dot(
        combine_weights, returned.reshape(slot_count, width), preferred_element_type=jnp.float32
    )
    slot_dot = jnp.sum(jnp.where(slot_hit, dot_sum.astype(jnp.float32)[None, :, :], 0.0), axis=2)
    gate_grad = jnp.sum(jnp.where(window_hit, slot_dot[:, None, :], 0.0), axis=2)
    chosen_grad = route_scale * (
        gate_grad / affin_sum
        - jnp.sum(gate_grad * chosen, axis=1, keepdims=True) / (affin_sum * affin_sum)
    )
    logit_pick = chosen_grad * chosen * (1.0 - chosen)
    logit_grad = jnp.sum(jnp.where(choose, logit_pick[:, :, None], 0.0), axis=1).astype(
        jnp.bfloat16
    )
    unit_grad = unit_grad + jnp.dot(logit_grad, router, preferred_element_type=jnp.float32)
    scaled = unit_grad * norm_gain
    residual_stream_gradient = (
        cotangent.astype(jnp.float32)
        + inverse * (scaled - normed * jnp.mean(scaled * normed, axis=1, keepdims=True))
    ).astype(jnp.bfloat16)
    hidden_code_gradient = (
        adapter_scale_factor
        * jnp.einsum(
            "td,rd->tr",
            residual_stream_gradient,
            adapter_raise_factor,
            preferred_element_type=jnp.float32,
        )
    ).astype(jnp.bfloat16)
    partial_raise_sum = adapter_scale_factor * jnp.einsum(
        "tr,td->rd", hidden_code, residual_stream_gradient, preferred_element_type=jnp.float32
    )
    part_down = jnp.einsum(
        "tr,th->rh", hidden_code_gradient, heads_out, preferred_element_type=jnp.float32
    )
    sum_down, sum_up = lax.psum((part_down, partial_raise_sum), ("dp", "expert"))
    device_group = replicas * experts_here
    return (residual_stream_gradient, sum_down / device_group, sum_up / device_group)


def solution(mesh):
    return jax.shard_map(
        local,
        mesh=mesh,
        in_specs=(
            P(("dp", "expert"), None),
            P(("dp", "expert"), None),
            P(("dp", "expert"), None),
            P(),
            P(),
            P(),
            P(),
            P(("dp", "expert"), None),
            P("expert", None, None, "dp"),
            P("expert", "dp", None),
        ),
        out_specs=(P(("dp", "expert"), None), P(), P()),
        check_vma=False,
    )
```

profile of v0, /device:TPU:1, one launch (start us, length us, event | category | flops | bytes accessed | tf_op | source)
XLA Modules:
  0.0 898.4 jit_solution(2683090951099843576)
XLA Ops:
  7.2 0.0 copy-start
  7.2 0.0 copy-start.6
  7.2 0.0 copy-start.7
  7.2 0.9 convert_reduce_fusion
  8.1 0.1 copy.71
  8.2 0.2 reduce_window_sum.11
  8.4 0.1 copy.73
  8.5 0.1 eq.76
  8.7 3.4 convolution_convert_fusion.3
  12.0 0.0 copy-done.7
  12.1 0.0 copy-start.8
  12.1 0.9 multiply_reduce_fusion.1
  13.0 0.0 copy-start.12
  13.0 0.1 compare_and_fusion
  13.1 1.8 copy-done.2
  14.9 1.0 convolution_convert_fusion.1
  15.9 2.7 broadcast_in_dim.107
  18.6 6.6 broadcast_in_dim.108
  25.2 11.9 %all-to-all-start.1 = ((bf16[128,6,7168]{2,1,0:T(8,128)(2,1)}), bf16[128,6,7168]{2,1,0:T(8,128)(2,1)}, u32[]{:S(2)}, u32[]{:S(2)}) async-start(bf16[128,6,7168]{2,1,0:T(8,128)(2,1)} %bitcast.39), calls=%async_computation.1 | async-start | bytes 29360128 | tf_op jit(solution)/shard_map/all_to_all | solution.py:99
  37.1 2.4 convolution_convert_fusion.2
  39.5 2.7 broadcast_in_dim.105
  42.2 188.8 %all-to-all-done.1 = bf16[128,6,7168]{2,1,0:T(8,128)(2,1)} async-done(((bf16[128,6,7168]{2,1,0:T(8,128)(2,1)}), bf16[128,6,7168]{2,1,0:T(8,128)(2,1)}, u32[]{:S(2)}, u32[]{:S(2)}) %all-to-all-start.1) | async-done | bytes 11010080 | tf_op jit(solution)/shard_map/all_to_all | solution.py:99
  230.9 6.6 broadcast_in_dim.106
  237.6 12.9 %all-to-all-start = ((bf16[128,6,7168]{2,1,0:T(8,128)(2,1)}), bf16[128,6,7168]{2,1,0:T(8,128)(2,1)}, u32[]{:S(2)}, u32[]{:S(2)}) async-start(bf16[128,6,7168]{2,1,0:T(8,128)(2,1)} %bitcast.38), calls=%async_computation | async-start | bytes 29360128 | tf_op jit(solution)/shard_map/all_to_all | solution.py:106
  250.5 12.4 %reshape.174 = bf16[7168,512,1]{1,0,2:T(8,128)(2,1)} reshape(bf16[1,7168,2,256]{3,2,1,0:T(2,128)(2,1)} %param.18) | data formatting | bytes 14680064 | tf_op jit(solution)/shard_map/reshape | solution.py:25
  262.9 7.3 copy.93
  270.2 16.4 %reshape.170 = bf16[768,7168]{1,0:T(8,128)(2,1)} reshape(bf16[128,6,7168]{2,1,0:T(8,128)(2,1)} %all-to-all-done.1) | data formatting | bytes 22020096 | tf_op jit(solution)/shard_map/reshape | solution.py:23
  286.6 10.7 %fusion.24 = f32[768,512]{1,0:T(8,128)S(1)} fusion(bf16[768,7168]{1,0:T(8,128)(2,1)} %reshape.170, bf16[7168,512]{1,0:T(8,128)(2,1)} %bitcast.41), kind=kOutput, calls=%fused_computation.64 | convolution fusion | flops 5637144576 | bytes 19922944 | tf_op jit(solution)/shard_map/dot_general | solution.py:27
  297.4 150.8 %all-to-all-done = bf16[128,6,7168]{2,1,0:T(8,128)(2,1)} async-done(((bf16[128,6,7168]{2,1,0:T(8,128)(2,1)}), bf16[128,6,7168]{2,1,0:T(8,128)(2,1)}, u32[]{:S(2)}, u32[]{:S(2)}) %all-to-all-start) | async-done | bytes 11010080 | tf_op jit(solution)/shard_map/all_to_all | solution.py:106
  448.2 16.2 %reshape.167 = bf16[768,7168]{1,0:T(8,128)(2,1)} reshape(bf16[128,6,7168]{2,1,0:T(8,128)(2,1)} %all-to-all-done) | data formatting | bytes 22020096 | tf_op jit(solution)/shard_map/reshape | solution.py:24
  464.4 8.5 multiply_reduce_fusion.2
  472.9 0.8 convert_element_type.87
  473.7 8.3 all-to-all-start.3
  482.0 0.1 concatenate.9
  482.2 0.1 copy.78
  482.3 0.1 concatenate.10
  482.4 0.1 copy.79
  482.5 9.2 %convolution_convert_fusion = bf16[128,6,7168]{2,0,1:T(8,128)(2,1)S(1)} fusion(bf16[7168,512,1]{1,0,2:T(8,128)(2,1)} %reshape.174, bf16[128,6,256]{2,0,1:T(8,128)(2,1)S(1)} %copy.79, bf16[128,6,256]{2,0,1:T(8,128)(2,1)S(1)} %copy.78), kind=kOutput, calls=%fused_computation | convolution fusion | flops 5644222464 | bytes 19136512 | tf_op jit(solution)/shard_map/mk,dk->md/dot_general | solution.py:42
  491.7 10.2 %copy.80 = bf16[128,6,7168]{2,1,0:T(8,128)(2,1)} copy(bf16[128,6,7168]{2,0,1:T(8,128)(2,1)S(1)} %convolution_convert_fusion) | data formatting | bytes 22020096 | tf_op jit(solution)/shard_map/convert_element_type | solution.py:119
  501.9 0.0 all-to-all-done.3
  501.9 10.2 %all-to-all-start.2 = ((bf16[128,6,7168]{2,1,0:T(8,128)(2,1)}), bf16[128,6,7168]{2,1,0:T(8,128)(2,1)}, u32[]{:S(2)}, u32[]{:S(2)}) async-start(bf16[128,6,7168]{2,1,0:T(8,128)(2,1)} %copy.80), calls=%async_computation.2 | async-start | bytes 29360128 | tf_op jit(solution)/shard_map/all_to_all | solution.py:118
  512.1 0.0 all-reduce.3.cloned.1.call-start
  512.1 0.1 copy.74
  512.2 4.5 fusion.7
  516.8 2.0 select_reduce_fusion
  518.8 0.1 copy.83
  518.9 0.1 reshape.173
  519.1 0.1 select_reduce_fusion.5
  519.3 0.1 copy.88
  519.4 0.4 select_reduce_fusion.2
  519.8 186.1 %all-to-all-done.2 = bf16[128,6,7168]{2,1,0:T(8,128)(2,1)} async-done(((bf16[128,6,7168]{2,1,0:T(8,128)(2,1)}), bf16[128,6,7168]{2,1,0:T(8,128)(2,1)}, u32[]{:S(2)}, u32[]{:S(2)}) %all-to-all-start.2) | async-done | bytes 11010080 | tf_op jit(solution)/shard_map/all_to_all | solution.py:118
  705.9 11.4 %reduce_sum.128 = bf16[32,6,7168]{2,1,0:T(8,128)(2,1)} reduce(bf16[4,32,6,7168]{3,2,1,0:T(8,128)(2,1)} %bitcast.3, bf16[]{:T(256)} %constant.31.clone.1), dimensions={0}, to_apply=%region_6.7 | reduce | flops 4128768 | bytes 13762562 | tf_op jit(solution)/shard_map/reduce_sum | solution.py:133
  717.3 4.1 convolution_bitcast_fusion
  721.5 0.0 copy-start.5
  721.5 3.6 multiply_reduce_fusion
  725.2 1.0 add_convert_fusion
  726.2 0.0 copy-start.4
  726.2 0.0 copy-start.1
  726.2 6.0 fusion.9
  732.2 1.1 convolution_multiply_fusion.1
  733.4 0.0 all-reduce.3.cloned.1.call-update
  733.4 154.1 %all-reduce.3.cloned.1.call-done = (f32[16,16384]{1,0:T(8,128)}, f32[16,7168]{1,0:T(8,128)}) async-done(((f32[16,16384]{1,0:T(8,128)}, f32[16,7168]{1,0:T(8,128)}), (f32[16,16384]{1,0:T(8,128)}, f32[16,7168]{1,0:T(8,128)})) %all-reduce.3.cloned.1.call-update) | async-done | bytes 1507344 | tf_op jit(solution)/shard_map/psum | solution.py:178
  887.5 2.3 broadcast_multiply_fusion
  889.8 1.8 broadcast_multiply_fusion.1
  (35 shorter events, 0.3 us)
Async XLA Ops:
  7.2 1.5 copy-start
  7.2 4.8 copy-start.6
  7.2 4.9 copy-start.7
  12.1 1.0 copy-start.10
  12.1 2.8 copy-start.8
  13.0 1.9 copy-start.2
  13.0 5.6 copy-start.12
  25.2 205.7 %all-to-all-start.1 = ((bf16[128,6,7168]{2,1,0:T(8,128)(2,1)}), bf16[128,6,7168]{2,1,0:T(8,128)(2,1)}, u32[]{:S(2)}, u32[]{:S(2)}) async-start(bf16[128,6,7168]{2,1,0:T(8,128)(2,1)} %bitcast.39), calls=%async_computation.1 | async-start | bytes 29360128 | tf_op jit(solution)/shard_map/all_to_all | solution.py:99
  237.6 210.6 %all-to-all-start = ((bf16[128,6,7168]{2,1,0:T(8,128)(2,1)}), bf16[128,6,7168]{2,1,0:T(8,128)(2,1)}, u32[]{:S(2)}, u32[]{:S(2)}) async-start(bf16[128,6,7168]{2,1,0:T(8,128)(2,1)} %bitcast.38), calls=%async_computation | async-start | bytes 29360128 | tf_op jit(solution)/shard_map/all_to_all | solution.py:106
  473.7 28.2 %all-to-all-start.3 = ((bf16[128,1,6]{2,1,0:T(2,128)(2,1)}), bf16[128,1,6]{2,1,0:T(2,128)(2,1)S(1)}, u32[]{:S(2)}, u32[]{:S(2)}) async-start(bf16[128,1,6]{2,1,0:T(2,128)(2,1)} %convert_element_type.87), calls=%async_computation.3 | async-start | bytes 131072 | tf_op jit(solution)/shard_map/all_to_all | solution.py:125
  501.9 10.2 %copy-start.9 = (s32[128,8]{0,1:T(8,128)S(1)}, s32[128,8]{0,1:T(8,128)}, u32[]{:S(2)}) copy-start(s32[128,8]{0,1:T(8,128)} %param.17) | copy-start | bytes 12292
  501.9 10.3 %copy-start.13 = (f32[128]{0:T(128)S(1)}, f32[128]{0:T(128)}, u32[]{:S(2)}) copy-start(f32[128]{0:T(128)} %copy-done.12) | copy-start | bytes 1540
  501.9 204.0 %all-to-all-start.2 = ((bf16[128,6,7168]{2,1,0:T(8,128)(2,1)}), bf16[128,6,7168]{2,1,0:T(8,128)(2,1)}, u32[]{:S(2)}, u32[]{:S(2)}) async-start(bf16[128,6,7168]{2,1,0:T(8,128)(2,1)} %copy.80), calls=%async_computation.2 | async-start | bytes 29360128 | tf_op jit(solution)/shard_map/all_to_all | solution.py:118
  512.1 375.4 %all-reduce.3.cloned.1.call-start = ((), (), s32[]{:S(2)}) async-start(), calls=%async_computation.4 | async-start | bytes 3014656 | tf_op jit(solution)/shard_map/psum | solution.py:178
  717.3 4.1 copy-start.3
  721.5 3.7 copy-start.5
  726.2 7.2 copy-start.4
  726.2 6.0 copy-start.11
  726.2 165.4 %copy-start.1 = (bf16[16,16384]{1,0:T(8,128)(2,1)S(1)}, bf16[16,16384]{1,0:T(8,128)(2,1)}, u32[]{:S(2)}) copy-start(bf16[16,16384]{1,0:T(8,128)(2,1)} %param.13) | copy-start | bytes 1572868
Sparse Core Ops, SparseCore 0:
  733.5 153.9 all-reduce.2
where the time goes:
time: 900 us; the launch traced here: 898 us
  waiting for transfers between devices  680 us (76%)
  local copies, waits for them, and re-layouts  85.1 us (9%)
  matrix products  55.5 us (6%)
  starting transfers between devices  43.3 us (5%)
  other arithmetic  20.3 us (2%)
  between operations  14.4 us (2%)
    all_to_all x1, waiting for transfers between devices, local(): lax.all_to_all(repeat_rows(send_in, replicas), ('dp', 'expert'), split_ax...  189 us
    all_to_all x1, waiting for transfers between devices, local(): lax.all_to_all(partial_rows.astype(jnp.bfloat16), ('dp', 'expert'), split...  186 us
    psum x1, waiting for transfers between devices, local(): lax.psum((part_down, partial_raise_sum), ('dp', 'expert'))  154 us
    all_to_all x1, waiting for transfers between devices, local(): lax.all_to_all(repeat_rows(send_grad, replicas), ('dp', 'expert'), split_...  151 us
    broadcast_in_dim x4, local copies, waits for them, and re-layouts, repeat_rows(): copies = jnp.broadcast_to(block[None], (count,) + block.shape)  18.7 us
  transfers between devices with their start and end apart: 5, of which 4 were waited for; matrix products, arithmetic and copies ran while one was open for 9% of the time, Pallas kernels for 0%

commit v1 on v0

v1 whole, which is shorter than its diff:
```python
import jax
import jax.numpy as jnp
from jax import lax
from jax.sharding import Mesh
from jax.sharding import PartitionSpec as P

ALL_EXP = 256
CAP = 6
WIN = 32
SLOTS = WIN * CAP
LANES = 128

adapter_scale_factor = 2.0
route_scale = 2.5
norm_eps = 1e-06

ALL = ("pa", "pb", "chip", "core")
PAIR = ("pb", "chip", "core")
CHIPS = ("pa", "pb", "chip")
N_Y = 4
N_E = 32
N_DEV = N_Y * N_E
F32 = jnp.float32
BF16 = jnp.bfloat16


def keeps(y, e):
    return (e % 2) == (0 if y in (0, 3) else 1)


KEEP = [(y, e) for y in range(N_Y) for e in range(N_E) if keeps(y, e)]
LEAVE = [(y, e) for y in range(N_Y) for e in range(N_E) if not keeps(y, e)]
FIRST_KEEP = [(y * N_E + e, (3 - y) * N_E + e) for y, e in KEEP]
FIRST_LEAVE = [(y * N_E + e, (y ^ 1) * N_E + (e ^ 1)) for y, e in LEAVE]
LAST = [(y * N_E + e, (3 - y) * N_E + e) for y, e in LEAVE]
TO_LEAVE = [(y * N_E + e, y * N_E + (e ^ 1)) for y, e in KEEP]
TO_KEEP = [(y * N_E + e, y * N_E + (e ^ 1)) for y, e in LEAVE]
CORES = [(i, i ^ 1) for i in range(N_DEV)]


def move(block, pairs):
    return lax.ppermute(block, ALL, pairs)


def exchange(rows):
    return lax.all_to_all(rows, PAIR, split_axis=0, concat_axis=0, tiled=True)


def pack(rows):
    return rows.reshape(2 * N_E, -1, LANES)


def unpack(block):
    return block.reshape(SLOTS, -1)


def stays():
    return lax.axis_index("core") == (lax.axis_index("pa") ^ lax.axis_index("pb"))


def own_block(block):
    return jnp.where(stays(), block, move(block, TO_LEAVE))


def gather_gate(block):
    first = move(block, FIRST_KEEP + FIRST_LEAVE)
    last = move(first, LAST)
    return [own_block(block), first, move(first, CORES), last]


def gather_down(block):
    kept = move(block, FIRST_KEEP)
    left = move(block, FIRST_LEAVE)
    last = move(left, LAST)
    first = jnp.where(stays(), kept, left)
    return [own_block(block), first, move(first, CORES), last]


def last_block(last):
    return jnp.where(stays(), move(last, TO_KEEP), last)


def hidden_share(rows_in, rows_grad, joined, lowered):
    quarter = lowered.shape[0]
    projected = jnp.dot(rows_in, joined, preferred_element_type=F32)
    gate_pre = projected[:, :quarter]
    up_pre = projected[:, quarter:]
    sigma_gate = jax.nn.sigmoid(gate_pre)
    activated = gate_pre * sigma_gate
    hidden = (activated * up_pre).astype(BF16)
    hidden_grad = jnp.einsum("md,hd->mh", rows_grad, lowered, preferred_element_type=F32)
    slot_dots = jnp.sum(hidden.astype(F32) * hidden_grad, axis=1)
    pre_grad = jnp.concatenate(
        [
            hidden_grad * up_pre * sigma_gate * (1.0 + gate_pre * (1.0 - sigma_gate)),
            hidden_grad * activated,
        ],
        axis=1,
    ).astype(BF16)
    returned = jnp.einsum("mk,dk->md", pre_grad, joined, preferred_element_type=F32)
    return returned, slot_dots


def expert_rows(rows_in, rows_grad, shares):
    returned, dots = 0.0, 0.0
    for joined, lowered in shares:
        part, slot_dots = hidden_share(rows_in, rows_grad, joined, lowered)
        returned = returned + part
        dots = dots + slot_dots
    return returned, dots


def local(
    stream,
    heads_out,
    cotangent,
    adapter_down,
    adapter_raise_factor,
    norm_gain,
    router,
    expert_ids,
    w_gate_up,
    w_down,
):
    tokens_here, width = stream.shape
    quarter = w_down.shape[1]
    pa = lax.axis_index("pa")

    joined = gather_gate(w_gate_up.reshape(width, 2, quarter))
    joined[:3] = [lax.optimization_barrier(j.reshape(width, 2 * quarter)) for j in joined[:3]]
    lowered = gather_down(w_down.reshape(quarter, width))

    place = jnp.arange(WIN, dtype=jnp.int32)
    order = 2 * (place % 16) + ((place // 16) ^ pa)
    window_hit = expert_ids[:, :, None] == order[None, None, :]
    member = jnp.sum(window_hit.astype(F32), axis=1)
    earlier = jnp.arange(tokens_here)[:, None] > jnp.arange(tokens_here)[None, :]
    position = jnp.dot(
        earlier.astype(BF16), member.astype(BF16), preferred_element_type=F32
    ).astype(jnp.int32)
    slot_hit = (member[:, :, None] == 1.0) & (
        position[:, :, None] == jnp.arange(CAP, dtype=jnp.int32)[None, None, :]
    )
    pick = slot_hit.reshape(tokens_here, SLOTS).astype(BF16)

    send_grad = pack(
        jnp.einsum("ts,td->sd", pick, cotangent, preferred_element_type=F32).astype(BF16)
    )
    hidden_code = jnp.einsum(
        "th,rh->tr", heads_out, adapter_down, preferred_element_type=F32
    ).astype(BF16)
    combined_result = stream.astype(F32) + adapter_scale_factor * jnp.dot(
        hidden_code, adapter_raise_factor, preferred_element_type=F32
    )
    inverse = lax.rsqrt(
        jnp.mean(combined_result * combined_result, axis=1, keepdims=True) + norm_eps
    )
    normed = combined_result * inverse
    normed_in = (normed * norm_gain).astype(BF16)
    send_in = pack(
        jnp.einsum("ts,td->sd", pick, normed_in, preferred_element_type=F32).astype(BF16)
    )
    send_grad, send_in, joined[0] = lax.optimization_barrier((send_grad, send_in, joined[0]))
    rows_grad = exchange(send_grad)
    send_in, rows_grad = lax.optimization_barrier((send_in, rows_grad))
    rows_in = exchange(send_in)

    logits = jnp.einsum("td,ed->te", normed_in, router, preferred_element_type=F32)
    affinity = jax.nn.sigmoid(logits)
    choose = expert_ids[:, :, None] == jnp.arange(ALL_EXP, dtype=jnp.int32)[None, None, :]
    chosen = jnp.sum(jnp.where(choose, affinity[:, None, :], 0.0), axis=2)
    affin_sum = jnp.sum(chosen, axis=1, keepdims=True)
    gate_weights = route_scale * chosen / affin_sum
    gate_window = jnp.sum(jnp.where(window_hit, gate_weights[:, :, None], 0.0), axis=1)
    combine_weights = (
        jnp.where(slot_hit, gate_window[:, :, None], 0.0)
        .reshape(tokens_here, SLOTS)
        .astype(BF16)
    )

    rows_in, joined[1], joined[2] = lax.optimization_barrier((rows_in, joined[1], joined[2]))
    rows_in, rows_grad = unpack(rows_in), unpack(rows_grad)
    shares = list(zip(joined, lowered))
    own_rows, own_dots = expert_rows(rows_in, rows_grad, shares[:1])
    own_dots, joined[3] = lax.optimization_barrier((own_dots, joined[3]))
    more_rows, more_dots = expert_rows(rows_in, rows_grad, shares[1:3])
    early_rows, early_dots = own_rows + more_rows, own_dots + more_dots
    early_rows = lax.optimization_barrier(early_rows)
    last_joined = last_block(joined[3]).reshape(width, 2 * quarter)
    last_joined = lax.optimization_barrier(last_joined)
    last_share = (last_joined, last_block(lowered[3]))
    late_rows, late_dots = hidden_share(rows_in, rows_grad, *last_share)
    back_rows = (early_rows + late_rows).astype(BF16)
    dots = early_dots + late_dots
    dots = dots.astype(BF16).reshape(2 * N_E, 1, 3)
    dots = jnp.pad(dots, ((0, 0), (0, 7), (0, LANES - 3)))
    back = exchange(jnp.concatenate([pack(back_rows), dots], axis=1))
    returned = unpack(back[:, :-8])
    dot_sum = back[:, -8, :3].reshape(WIN, CAP)

    slot_dot = jnp.sum(jnp.where(slot_hit, dot_sum.astype(F32)[None, :, :], 0.0), axis=2)
    gate_grad = jnp.sum(jnp.where(window_hit, slot_dot[:, None, :], 0.0), axis=2)
    chosen_grad = route_scale * (
        gate_grad / affin_sum
        - jnp.sum(gate_grad * chosen, axis=1, keepdims=True) / (affin_sum * affin_sum)
    )
    logit_pick = chosen_grad * chosen * (1.0 - chosen)
    logit_grad = jnp.sum(jnp.where(choose, logit_pick[:, :, None], 0.0), axis=1).astype(BF16)
    router_grad = jnp.dot(logit_grad, router, preferred_element_type=F32)

    unit_grad = jnp.dot(combine_weights, returned, preferred_element_type=F32) + router_grad
    scaled = unit_grad * norm_gain
    residual_stream_gradient = (
        cotangent.astype(F32)
        + inverse * (scaled - normed * jnp.mean(scaled * normed, axis=1, keepdims=True))
    ).astype(BF16)
    hidden_code_gradient = (
        adapter_scale_factor
        * jnp.einsum(
            "td,rd->tr", residual_stream_gradient, adapter_raise_factor, preferred_element_type=F32
        )
    ).astype(BF16)
    raise_part = (adapter_scale_factor / N_DEV) * jnp.einsum(
        "tr,td->rd", hidden_code, residual_stream_gradient, preferred_element_type=F32
    )
    down_part = (1.0 / N_DEV) * jnp.einsum(
        "tr,th->rh", hidden_code_gradient, heads_out, preferred_element_type=F32
    )

    rank = adapter_down.shape[0]
    down_cut = down_part.astype(BF16).reshape(rank, N_DEV, LANES).transpose(1, 0, 2)
    raise_cut = raise_part.astype(BF16).reshape(N_DEV, 7, LANES)
    raise_cut = jnp.pad(raise_cut, ((0, 0), (0, 1), (0, 0)))
    cut = jnp.concatenate([down_cut, raise_cut], axis=1)
    core = lax.axis_index("core")
    cut = cut.reshape(N_DEV // 2, 2, -1, LANES)
    mine = jnp.where(core == 0, cut[:, 0], cut[:, 1])
    other = move(jnp.where(core == 0, cut[:, 1], cut[:, 0]), CORES)
    cut = (mine.astype(F32) + other.astype(F32)).astype(BF16)
    cut = lax.all_to_all(cut, CHIPS, split_axis=0, concat_axis=0, tiled=True)
    total = jnp.sum(cut.astype(F32), axis=0).astype(BF16)
    half = jnp.broadcast_to(total[None], cut.shape)
    half = lax.all_to_all(half, CHIPS, split_axis=0, concat_axis=0, tiled=True)
    other = move(half, CORES)
    whole = jnp.stack(
        [jnp.where(core == 0, half, other), jnp.where(core == 0, other, half)], axis=1
    ).reshape(N_DEV, -1, LANES)
    sum_down = whole[:, :rank].transpose(1, 0, 2).reshape(rank, N_DEV * LANES).astype(F32)
    sum_up = whole[:, rank : rank + 7].reshape(rank, width).astype(F32)
    return (residual_stream_gradient, sum_down, sum_up)


def solution(mesh):
    wide = Mesh(mesh.devices.reshape(2, 2, N_E // 2, 2), ALL)
    return jax.shard_map(
        local,
        mesh=wide,
        in_specs=(
            P(ALL, None),
            P(ALL, None),
            P(ALL, None),
            P(),
            P(),
            P(),
            P(),
            P(ALL, None),
            P(("chip", "core"), None, None, ("pa", "pb")),
            P(("chip", "core"), ("pa", "pb"), None),
        ),
        out_specs=(P(ALL, None), P(), P()),
        check_vma=False,
    )
```

time: 900 us -> 443 us (0.49)
  waiting for transfers between devices: 680 us -> 188 us
  blocking collectives: 0 us -> 33.2 us
  local copies, waits for them, and re-layouts: 85.1 us -> 55.9 us
  starting transfers between devices: 43.3 us -> 60.6 us
  between operations: 14.4 us -> 1.77 us
  matrix products: 55.5 us -> 65.8 us
    all_to_all x4 -> x3, waiting for transfers between devices: 526 us -> 59.9 us  [exchange(): return lax.all_to_all(rows, PAIR, split_axis=0, concat_axis=0, tiled=True)]
    psum x1 -> x0, waiting for transfers between devices: 154 us -> none  [local(): lax.psum((part_down, partial_raise_sum), ('dp', 'expert'))]
    ppermute x0 -> x13, waiting for transfers between devices: none -> 129 us  [move(): return lax.ppermute(block, ALL, pairs)]
    ppermute x0 -> x13, starting transfers between devices: none -> 34.2 us  [move(): return lax.ppermute(block, ALL, pairs)]
    all_to_all x0 -> x2, blocking collectives: none -> 33.2 us  [the longest x1 18.5 us: local(): cut = lax.all_to_all(cut, CHIPS, split_axis=0, concat_axis=0, tiled=True)]
    reshape x4 -> x9, local copies, waits for them, and re-layouts: 45.1 us -> 23 us  [the longest x3 11.8 us: unpack(): return block.reshape(SLOTS, -1)]
    unnamed x30 -> x51, local copies, waits for them, and re-layouts: 9.29 us -> 29.8 us
    broadcast_in_dim x4 -> x1, local copies, waits for them, and re-layouts: 18.7 us -> 0.05 us  [local(): half = jnp.broadcast_to(total[None], cut.shape)]
  transfers between devices with their start and end apart: 5 -> 16, of which waited for: 4 -> 7; matrix products, arithmetic and copies ran while one was open for 9% -> 26% of each run, Pallas kernels for 0% -> 0%
where the time goes in v1:
time: 443 us; the launch traced here: 434 us
  waiting for transfers between devices  188 us (42%)
  matrix products  65.8 us (15%)
  starting transfers between devices  60.6 us (14%)
  local copies, waits for them, and re-layouts  55.9 us (13%)
  blocking collectives  33.2 us (7%)
  other arithmetic  28.5 us (6%)
    ppermute x13, waiting for transfers between devices, move(): return lax.ppermute(block, ALL, pairs)  129 us
    all_to_all x3, waiting for transfers between devices, exchange(): return lax.all_to_all(rows, PAIR, split_axis=0, concat_axis=0, tiled=True)  59.9 us
    ppermute x13, starting transfers between devices, move(): return lax.ppermute(block, ALL, pairs)  34.2 us
    unnamed x51, local copies, waits for them, and re-layouts  29.8 us
    all_to_all x3, starting transfers between devices, exchange(): return lax.all_to_all(rows, PAIR, split_axis=0, concat_axis=0, tiled=True)  26.4 us
    all_to_all x1, blocking collectives, local(): cut = lax.all_to_all(cut, CHIPS, split_axis=0, concat_axis=0, tiled=True)  18.5 us
    dot_general x4, matrix products, hidden_share(): jnp.einsum('mk,dk->md', pre_grad, joined, preferred_element_type=F32)  16.3 us
    dot_general x4, matrix products, hidden_share(): projected = jnp.dot(rows_in, joined, preferred_element_type=F32)  15.4 us
  transfers between devices with their start and end apart: 16, of which 7 were waited for; matrix products, arithmetic and copies ran while one was open for 26% of the time, Pallas kernels for 0%

profile of v1, /device:TPU:1, one launch (start us, length us, event | category | flops | bytes accessed | tf_op | source)
XLA Modules:
  0.0 434.3 jit_solution(13719151186012147981)
XLA Ops:
  0.7 2.8 collective-permute-start.2
  3.4 1.3 collective-permute-start
  5.9 3.4 convolution_convert_fusion.3
  9.3 0.9 multiply_reduce_fusion.1
  10.3 1.8 copy-done.2
  12.1 1.0 convolution_convert_fusion
  13.1 70.8 %collective-permute-done.2 = bf16[7168,2,256]{2,1,0:T(2,128)(2,1)} collective-permute-done((bf16[7168,2,256]{2,1,0:T(2,128)(2,1)}, bf16[7168,2,256]{2,1,0:T(2,128)(2,1)}, u32[]{:S(2)}, u32[]{:S(2)}) %collective-permute-start.2) | collective-permute-done | bytes 7340064 | tf_op jit(solution)/shard_map/ppermute | solution.py:42
  83.9 1.9 collective-permute-start.3
  85.9 2.4 convolution_convert_fusion.1
  88.3 2.7 reshape.232
  91.0 5.3 %reshape.231 = bf16[64,168,128]{2,1,0:T(8,128)(2,1)} reshape(bf16[192,7168]{1,0:T(8,128)(2,1)} %convolution_convert_fusion.1) | data formatting | bytes 5505024 | tf_op jit(solution)/shard_map/reshape | solution.py:50
  96.3 4.7 %collective-permute-start.9 = (bf16[7168,2,256]{2,1,0:T(2,128)(2,1)}, bf16[7168,2,256]{2,1,0:T(2,128)(2,1)}, u32[]{:S(2)}, u32[]{:S(2)}) collective-permute-start(bf16[7168,2,256]{2,1,0:T(2,128)(2,1)} %collective-permute-done.2), channel_id=1, source_target_pairs={{1,97},{3,99},{5,101},{7,103},{9,105},{11,107},{13,109},{15,111},{... | collective-permute-start | bytes 22020104 | tf_op jit(solution)/shard_map/ppermute | solution.py:42
  101.1 9.2 %broadcast_select_fusion.1 = bf16[7168,2,256]{2,1,0:T(2,128)(2,1)S(1)} fusion(bf16[7168,2,256]{2,1,0:T(2,128)(2,1)} %collective-permute-done, pred[]{:T(512)S(6)} %eq.100, bf16[1,7168,2,256]{3,2,1,0:T(2,128)(2,1)} %param.18), kind=kLoop, calls=%fused_computation.3 | loop fusion | flops 3670016 | bytes 22020096 | tf_op jit(solution)/shard_map/jit(_where)/select_n | solution.py:62
  110.3 4.2 copy.68
  114.5 8.4 %all-to-all-start = ((bf16[64,168,128]{2,1,0:T(8,128)(2,1)}), bf16[64,168,128]{2,1,0:T(8,128)(2,1)S(1)}, u32[]{:S(2)}, u32[]{:S(2)}) async-start(bf16[64,168,128]{2,1,0:T(8,128)(2,1)} %reshape.231), calls=%async_computation | async-start | bytes 5505024 | tf_op jit(solution)/shard_map/all_to_all | solution.py:46
  122.9 3.6 collective-permute-start.5
  126.6 1.3 collective-permute-start.1
  127.9 30.2 %all-to-all-done = bf16[64,168,128]{2,1,0:T(8,128)(2,1)S(1)} async-done(((bf16[64,168,128]{2,1,0:T(8,128)(2,1)}), bf16[64,168,128]{2,1,0:T(8,128)(2,1)S(1)}, u32[]{:S(2)}, u32[]{:S(2)}) %all-to-all-start) | async-done | bytes 2752544 | tf_op jit(solution)/shard_map/all_to_all | solution.py:46
  158.1 7.0 %all-to-all-start.1 = ((bf16[64,168,128]{2,1,0:T(8,128)(2,1)}), bf16[64,168,128]{2,1,0:T(8,128)(2,1)}, u32[]{:S(2)}, u32[]{:S(2)}) async-start(bf16[64,168,128]{2,1,0:T(8,128)(2,1)} %reshape.232), calls=%async_computation.1 | async-start | bytes 5505024 | tf_op jit(solution)/shard_map/all_to_all | solution.py:46
  165.0 2.4 collective-permute-start.4
  167.4 52.8 %collective-permute-done.5 = bf16[256,7168]{1,0:T(8,128)(2,1)} collective-permute-done((bf16[256,7168]{1,0:T(8,128)(2,1)}, bf16[256,7168]{1,0:T(8,128)(2,1)}, u32[]{:S(2)}, u32[]{:S(2)}) %collective-permute-start.5) | collective-permute-done | bytes 3670048 | tf_op jit(solution)/shard_map/ppermute | solution.py:42
  220.2 3.8 collective-permute-start.7
  224.0 7.3 %copy.69 = bf16[896,8,2,256]{3,1,2,0:T(8,128)(2,1)} copy(bf16[896,8,2,256]{3,2,1,0:T(2,128)(2,1)} %bitcast.22) | data formatting | bytes 14680064
  231.4 2.6 reshape.235
  234.0 7.4 %copy.70 = bf16[896,8,2,256]{3,1,2,0:T(8,128)(2,1)} copy(bf16[896,8,2,256]{3,2,1,0:T(2,128)(2,1)} %bitcast.24) | data formatting | bytes 14680064
  241.4 5.3 %reshape.239 = bf16[192,7168]{1,0:T(8,128)(2,1)} reshape(bf16[64,168,128]{2,1,0:T(8,128)(2,1)} %all-to-all-done.1) | data formatting | bytes 5505024 | tf_op jit(solution)/shard_map/reshape | solution.py:54
  246.7 5.6 %fusion.55 = f32[192,512]{1,0:T(8,128)S(1)} fusion(bf16[192,7168]{1,0:T(8,128)(2,1)} %reshape.239, bf16[7168,512]{1,0:T(8,128)(2,1)} %bitcast.98), kind=kOutput, calls=%fused_computation.131 | convolution fusion | flops 1409286144 | bytes 10485760 | tf_op jit(solution)/shard_map/dot_general | solution.py:85
  252.4 3.7 multiply_convert_fusion.12
  256.1 4.6 %collective-permute-start.10 = (bf16[7168,2,256]{2,1,0:T(2,128)(2,1)}, bf16[7168,2,256]{2,1,0:T(2,128)(2,1)}, u32[]{:S(2)}, u32[]{:S(2)}) collective-permute-start(bf16[7168,2,256]{2,1,0:T(2,128)(2,1)} %collective-permute-done.9), channel_id=1, source_target_pairs={{1,0},{3,2},{5,4},{7,6},{9,8},{11,10},{13,12},{15,14},{17,16},{19,... | collective-permute-start | bytes 22020104 | tf_op jit(solution)/shard_map/ppermute | solution.py:42
  260.7 2.4 broadcast_select_fusion.2
  263.2 2.2 collective-permute-done.7
  265.4 3.3 collective-permute-start.8
  268.8 1.6 fusion.56
  270.4 1.5 multiply_convert_fusion.10
  271.8 2.5 fusion.24
  274.4 3.4 fusion.57
  277.8 3.5 multiply_convert_fusion.8
  281.3 5.6 %convolution_add_fusion.1 = f32[192,7168]{1,0:T(8,128)S(1)} fusion(f32[192,7168]{1,0:T(8,128)S(1)} %fusion.24, bf16[7168,512]{1,0:T(8,128)(2,1)} %bitcast.100, bf16[192,256]{1,0:T(8,128)(2,1)S(1)} %get-tuple-element.37, bf16[192,256]{1,0:T(8,128)(2,1)S(1)} %get-tuple-element.35), kind=kOutput, calls=%fused_computation.5 | convolution fusion | flops 1411055616 | bytes 18546688 | tf_op jit(solution)/shard_map/mk,dk->md/dot_general | solution.py:100
  286.9 5.6 %convolution_add_fusion.2 = f32[192,7168]{1,0:T(8,128)S(1)} fusion(f32[192,7168]{1,0:T(8,128)S(1)} %convolution_add_fusion.1, bf16[7168,512]{1,0:T(8,128)(2,1)} %bitcast.99, bf16[192,256]{1,0:T(8,128)(2,1)S(1)} %get-tuple-element.34, bf16[192,256]{1,0:T(8,128)(2,1)S(1)} %get-tuple-element.32), kind=kOutput, calls=%fused_computation.6 | convolution fusion | flops 1411055616 | bytes 18546688 | tf_op jit(solution)/shard_map/mk,dk->md/dot_general | solution.py:100
  292.5 6.9 %broadcast_select_fusion = bf16[1792,8,256]{2,1,0:T(8,128)(2,1)} fusion(bf16[1792,8,256]{2,1,0:T(8,128)(2,1)} %bitcast.85, bf16[1792,8,256]{2,1,0:T(8,128)(2,1)} %bitcast.86, pred[]{:T(512)S(6)} %eq.100), kind=kLoop, calls=%fused_computation.2 | loop fusion | flops 3670016 | bytes 22020096 | tf_op jit(solution)/shard_map/jit(_where)/select_n | solution.py:80
  299.4 7.5 %copy.71 = bf16[896,8,2,256]{3,1,2,0:T(8,128)(2,1)} copy(bf16[896,8,2,256]{3,2,1,0:T(2,128)(2,1)} %bitcast.96) | data formatting | bytes 14680064
  306.8 4.8 %fusion.58 = f32[192,512]{1,0:T(8,128)S(1)} fusion(bf16[192,7168]{1,0:T(8,128)(2,1)S(1)} %copy-done.10, bf16[7168,512]{1,0:T(8,128)(2,1)} %bitcast.92), kind=kOutput, calls=%fused_computation.134 | convolution fusion | flops 1409286144 | bytes 10485760 | tf_op jit(solution)/shard_map/dot_general | solution.py:85
  311.7 3.5 multiply_convert_fusion.5
  315.2 2.6 fusion.1
  317.8 2.7 reshape.241
  320.6 3.6 fusion.12
  324.2 11.1 %all-to-all-start.2 = ((bf16[64,176,128]{2,1,0:T(8,128)(2,1)}), bf16[64,176,128]{2,1,0:T(8,128)(2,1)S(1)}, u32[]{:S(2)}, u32[]{:S(2)}) async-start(bf16[64,176,128]{2,1,0:T(8,128)(2,1)} %fusion.12), calls=%async_computation.2 | async-start | bytes 5767168 | tf_op jit(solution)/shard_map/all_to_all | solution.py:46
  335.4 4.5 %fusion.17 = f32[128,256]{1,0:T(8,128)S(1)} fusion(bf16[256,7168]{1,0:T(8,128)(2,1)} %param.16, f32[128,7168]{1,0:T(8,128)} %copy-done.2, f32[7168]{0:T(1024)S(1)} %copy-done.14, f32[128]{0:T(128)S(1)} %add_rsqrt_fusion), kind=kOutput, calls=%fused_computation.38 | convolution fusion | flops 472612864 | bytes 7500288 | tf_op jit(solution)/shard_map/td,ed->te/dot_general | solution.py:168
  339.9 2.0 select_reduce_fusion
  342.0 29.7 %all-to-all-done.2 = bf16[64,176,128]{2,1,0:T(8,128)(2,1)S(1)} async-done(((bf16[64,176,128]{2,1,0:T(8,128)(2,1)}), bf16[64,176,128]{2,1,0:T(8,128)(2,1)S(1)}, u32[]{:S(2)}, u32[]{:S(2)}) %all-to-all-start.2) | async-done | bytes 2883616 | tf_op jit(solution)/shard_map/all_to_all | solution.py:46
  372.7 1.7 slice.66
  374.4 3.9 reshape.243
  379.1 1.4 copy-done.3
  380.4 3.6 multiply_reduce_fusion
  384.1 1.0 add_convert_fusion
  385.2 5.0 %fusion.14 = bf16[2,128,8,128]{3,2,1,0:T(8,128)(2,1)S(1)} fusion(bf16[128,16384]{1,0:T(8,128)(2,1)} %param.11, bf16[128,7168]{1,0:T(8,128)(2,1)S(1)} %add_convert_fusion, bf16[16,7168]{1,0:T(8,128)(2,1)S(1)} %copy-done.13), kind=kOutput, calls=%fused_computation.34 | convolution fusion | flops 96997376 | bytes 6782976 | tf_op jit(solution)/shard_map/tr,th->rh/dot_general | solution.py:226
  391.2 1.1 collective-permute-start.11
  392.3 1.3 collective-permute-done.11
  393.8 18.5 %all_to_all.25 = bf16[64,24,128]{2,1,0:T(8,128)(2,1)S(1)} all-to-all(bf16[64,24,128]{2,1,0:T(8,128)(2,1)S(1)} %fusion.20), channel_id=1, replica_groups=mesh['pa'=2,'pb'=2,'chip'=16,'core'=2] {'pa','pb','chip'}, dimensions={0} | all-to-all | bytes 786432 | tf_op jit(solution)/shard_map/all_to_all | solution.py:240
  412.5 14.7 %all_to_all.26 = bf16[64,24,128]{2,1,0:T(8,128)(2,1)S(1)} all-to-all(bf16[64,24,128]{2,1,0:T(8,128)(2,1)S(1)} %broadcast_in_dim.102), channel_id=1, replica_groups=mesh['pa'=2,'pb'=2,'chip'=16,'core'=2] {'pa','pb','chip'}, dimensions={0} | all-to-all | bytes 786432 | tf_op jit(solution)/shard_map/all_to_all | solution.py:243
  427.2 3.2 collective-permute-start.12
  430.4 1.3 collective-permute-done.12
  431.9 1.0 copy_bitcast_fusion
  433.0 0.9 reshape.251
  (98 shorter events, 4.9 us)
Async XLA Ops:
  0.6 5.3 %copy-start = (bf16[16,16384]{1,0:T(8,128)(2,1)S(1)}, bf16[16,16384]{1,0:T(8,128)(2,1)}, u32[]{:S(2)}) copy-start(bf16[16,16384]{1,0:T(8,128)(2,1)} %param.13) | copy-start | bytes 1572868
  0.6 8.6 %copy-start.11 = (bf16[128,7168]{1,0:T(8,128)(2,1)S(1)}, bf16[128,7168]{1,0:T(8,128)(2,1)}, u32[]{:S(2)}) copy-start(bf16[128,7168]{1,0:T(8,128)(2,1)} %param.10) | copy-start | bytes 5505028
  0.7 8.6 %copy-start.12 = (bf16[16,7168]{1,0:T(8,128)(2,1)S(1)}, bf16[16,7168]{1,0:T(8,128)(2,1)}, u32[]{:S(2)}) copy-start(bf16[16,7168]{1,0:T(8,128)(2,1)} %param.14) | copy-start | bytes 688132
  0.7 83.3 %collective-permute-start.2 = (bf16[7168,2,256]{2,1,0:T(2,128)(2,1)}, bf16[7168,2,256]{2,1,0:T(2,128)(2,1)}, u32[]{:S(2)}, u32[]{:S(2)}) collective-permute-start(bf16[7168,2,256]{2,1,0:T(2,128)(2,1)} %bitcast.104), channel_id=1, source_target_pairs={{0,96},{2,98},{4,100},{6,102},{8,104},{10,106},{12,108},{14,110},{... | collective-permute-start | bytes 22020104 | tf_op jit(solution)/shard_map/ppermute | solution.py:42
  3.4 97.6 %collective-permute-start = (bf16[7168,2,256]{2,1,0:T(2,128)(2,1)}, bf16[7168,2,256]{2,1,0:T(2,128)(2,1)}, u32[]{:S(2)}, u32[]{:S(2)}) collective-permute-start(bf16[7168,2,256]{2,1,0:T(2,128)(2,1)} %bitcast.105), channel_id=1, source_target_pairs={{0,1},{2,3},{4,5},{6,7},{8,9},{10,11},{12,13},{14,15},{16,17},{18,... | collective-permute-start | bytes 22020104 | tf_op jit(solution)/shard_map/ppermute | solution.py:42
  9.3 2.8 copy-start.14
  10.2 1.9 copy-start.2
  10.2 75.7 %copy-start.5 = (bf16[128,7168]{1,0:T(8,128)(2,1)S(1)}, bf16[128,7168]{1,0:T(8,128)(2,1)}, u32[]{:S(2)}) copy-start(bf16[128,7168]{1,0:T(8,128)(2,1)} %param.12) | copy-start | bytes 5505028
  83.9 150.0 %collective-permute-start.3 = (bf16[7168,2,256]{2,1,0:T(2,128)(2,1)}, bf16[7168,2,256]{2,1,0:T(2,128)(2,1)}, u32[]{:S(2)}, u32[]{:S(2)}) collective-permute-start(bf16[7168,2,256]{2,1,0:T(2,128)(2,1)} %collective-permute-done.2), channel_id=1, source_target_pairs={{0,1},{1,0},{2,3},{3,2},{4,5},{5,4},{6,7},{7,6},{8,9},{9,8},{10,11... | collective-permute-start | bytes 22020104 | tf_op jit(solution)/shard_map/ppermute | solution.py:42
  96.3 159.8 %collective-permute-start.9 = (bf16[7168,2,256]{2,1,0:T(2,128)(2,1)}, bf16[7168,2,256]{2,1,0:T(2,128)(2,1)}, u32[]{:S(2)}, u32[]{:S(2)}) collective-permute-start(bf16[7168,2,256]{2,1,0:T(2,128)(2,1)} %collective-permute-done.2), channel_id=1, source_target_pairs={{1,97},{3,99},{5,101},{7,103},{9,105},{11,107},{13,109},{15,111},{... | collective-permute-start | bytes 22020104 | tf_op jit(solution)/shard_map/ppermute | solution.py:42
  114.5 43.6 %all-to-all-start = ((bf16[64,168,128]{2,1,0:T(8,128)(2,1)}), bf16[64,168,128]{2,1,0:T(8,128)(2,1)S(1)}, u32[]{:S(2)}, u32[]{:S(2)}) async-start(bf16[64,168,128]{2,1,0:T(8,128)(2,1)} %reshape.231), calls=%async_computation | async-start | bytes 5505024 | tf_op jit(solution)/shard_map/all_to_all | solution.py:46
  122.9 97.3 %collective-permute-start.5 = (bf16[256,7168]{1,0:T(8,128)(2,1)}, bf16[256,7168]{1,0:T(8,128)(2,1)}, u32[]{:S(2)}, u32[]{:S(2)}) collective-permute-start(bf16[256,7168]{1,0:T(8,128)(2,1)} %bitcast.111), channel_id=1, source_target_pairs={{1,32},{3,34},{5,36},{7,38},{9,40},{11,42},{13,44},{15,46},{17,48}... | collective-permute-start | bytes 11010056 | tf_op jit(solution)/shard_map/ppermute | solution.py:42
  126.6 125.8 %collective-permute-start.1 = (bf16[256,7168]{1,0:T(8,128)(2,1)}, bf16[256,7168]{1,0:T(8,128)(2,1)}, u32[]{:S(2)}, u32[]{:S(2)}) collective-permute-start(bf16[256,7168]{1,0:T(8,128)(2,1)} %bitcast.112), channel_id=1, source_target_pairs={{0,1},{2,3},{4,5},{6,7},{8,9},{10,11},{12,13},{14,15},{16,17},{18,... | collective-permute-start | bytes 11010056 | tf_op jit(solution)/shard_map/ppermute | solution.py:42
  158.1 83.3 %all-to-all-start.1 = ((bf16[64,168,128]{2,1,0:T(8,128)(2,1)}), bf16[64,168,128]{2,1,0:T(8,128)(2,1)}, u32[]{:S(2)}, u32[]{:S(2)}) async-start(bf16[64,168,128]{2,1,0:T(8,128)(2,1)} %reshape.232), calls=%async_computation.1 | async-start | bytes 5505024 | tf_op jit(solution)/shard_map/all_to_all | solution.py:46
  165.0 95.7 %collective-permute-start.4 = (bf16[256,7168]{1,0:T(8,128)(2,1)}, bf16[256,7168]{1,0:T(8,128)(2,1)}, u32[]{:S(2)}, u32[]{:S(2)}) collective-permute-start(bf16[256,7168]{1,0:T(8,128)(2,1)} %bitcast.113), channel_id=1, source_target_pairs={{0,96},{2,98},{4,100},{6,102},{8,104},{10,106},{12,108},{14,110},{... | collective-permute-start | bytes 11010056 | tf_op jit(solution)/shard_map/ppermute | solution.py:42
  220.2 45.1 %collective-permute-start.7 = (bf16[256,7168]{1,0:T(8,128)(2,1)}, bf16[256,7168]{1,0:T(8,128)(2,1)}, u32[]{:S(2)}, u32[]{:S(2)}) collective-permute-start(bf16[256,7168]{1,0:T(8,128)(2,1)} %collective-permute-done.5), channel_id=1, source_target_pairs={{1,97},{3,99},{5,101},{7,103},{9,105},{11,107},{13,109},{15,111},{... | collective-permute-start | bytes 11010056 | tf_op jit(solution)/shard_map/ppermute | solution.py:42
  246.7 5.7 %copy-start.7 = (bf16[192,7168]{1,0:T(8,128)(2,1)S(1)}, bf16[192,7168]{1,0:T(8,128)(2,1)}, u32[]{:S(2)}) copy-start(bf16[192,7168]{1,0:T(8,128)(2,1)} %reshape.235) | copy-start | bytes 8257540
  246.7 5.8 %copy-start.16 = (bf16[1,256,7168]{2,1,0:T(8,128)(2,1)S(1)}, bf16[1,256,7168]{2,1,0:T(8,128)(2,1)}, u32[]{:S(2)}) copy-start(bf16[1,256,7168]{2,1,0:T(8,128)(2,1)} %param.19) | copy-start | bytes 11010052
  246.7 22.1 %slice-start = ((s8[7340032]{0:T(1024)(128)(4,1)}), s8[4194304]{0:T(1024)(128)(4,1)S(1)}, s32[]{:S(2)}) async-start(s8[7340032]{0:T(1024)(128)(4,1)} %bitcast.88), calls=%async_computation.5 | async-start | bytes 8388608
  252.3 16.4 %slice-start.1 = ((s8[7340032]{0:T(1024)(128)(4,1)}), s8[3145728]{0:T(1024)(128)(4,1)S(1)}, s32[]{:S(2)}) async-start(s8[7340032]{0:T(1024)(128)(4,1)} %bitcast.88), calls=%async_computation.6 | async-start | bytes 6291456
  256.1 12.6 %copy-start.9 = (bf16[192,7168]{1,0:T(8,128)(2,1)S(1)}, bf16[192,7168]{1,0:T(8,128)(2,1)}, u32[]{:S(2)}) copy-start(bf16[192,7168]{1,0:T(8,128)(2,1)} %reshape.239) | copy-start | bytes 8257540
  256.1 36.3 %collective-permute-start.10 = (bf16[7168,2,256]{2,1,0:T(2,128)(2,1)}, bf16[7168,2,256]{2,1,0:T(2,128)(2,1)}, u32[]{:S(2)}, u32[]{:S(2)}) collective-permute-start(bf16[7168,2,256]{2,1,0:T(2,128)(2,1)} %collective-permute-done.9), channel_id=1, source_target_pairs={{1,0},{3,2},{5,4},{7,6},{9,8},{11,10},{13,12},{15,14},{17,16},{19,... | collective-permute-start | bytes 22020104 | tf_op jit(solution)/shard_map/ppermute | solution.py:42
  263.1 14.6 %collective-permute-start.6 = (bf16[256,7168]{1,0:T(8,128)(2,1)S(1)}, bf16[256,7168]{1,0:T(8,128)(2,1)}, u32[]{:S(2)}, u32[]{:S(2)}) collective-permute-start(bf16[256,7168]{1,0:T(8,128)(2,1)S(1)} %broadcast_select_fusion.2), channel_id=1, source_target_pairs={{0,1},{1,0},{2,3},{3,2},{4,5},{5,4},{6,7},{7,6},{8,9},{9,8},{10,11... | collective-permute-start | bytes 11010056 | tf_op jit(solution)/shard_map/ppermute | solution.py:42
  265.4 46.3 %collective-permute-start.8 = (bf16[256,7168]{1,0:T(8,128)(2,1)}, bf16[256,7168]{1,0:T(8,128)(2,1)}, u32[]{:S(2)}, u32[]{:S(2)}) collective-permute-start(bf16[256,7168]{1,0:T(8,128)(2,1)} %collective-permute-done.7), channel_id=1, source_target_pairs={{1,0},{3,2},{5,4},{7,6},{9,8},{11,10},{13,12},{15,14},{17,16},{19,... | collective-permute-start | bytes 11010056 | tf_op jit(solution)/shard_map/ppermute | solution.py:42
  270.4 4.0 slice-start.4
  271.8 2.5 slice-start.5
  299.4 7.5 %copy-start.10 = (bf16[192,7168]{1,0:T(8,128)(2,1)S(1)}, bf16[192,7168]{1,0:T(8,128)(2,1)}, u32[]{:S(2)}) copy-start(bf16[192,7168]{1,0:T(8,128)(2,1)} %reshape.239) | copy-start | bytes 8257540
  306.8 8.4 %slice-start.2 = ((s8[7340032]{0:T(1024)(128)(4,1)}), s8[4194304]{0:T(1024)(128)(4,1)S(1)}, s32[]{:S(2)}) async-start(s8[7340032]{0:T(1024)(128)(4,1)} %bitcast.93), calls=%async_computation.7 | async-start | bytes 8388608
  306.8 4.8 %copy-start.8 = (bf16[192,7168]{1,0:T(8,128)(2,1)S(1)}, bf16[192,7168]{1,0:T(8,128)(2,1)}, u32[]{:S(2)}) copy-start(bf16[192,7168]{1,0:T(8,128)(2,1)} %reshape.235) | copy-start | bytes 8257540
  306.8 8.4 %slice-start.3 = ((s8[7340032]{0:T(1024)(128)(4,1)}), s8[3145728]{0:T(1024)(128)(4,1)S(1)}, s32[]{:S(2)}) async-start(s8[7340032]{0:T(1024)(128)(4,1)} %bitcast.93), calls=%async_computation.8 | async-start | bytes 6291456
  324.2 11.1 %copy-start.15 = (s32[128,8]{0,1:T(8,128)S(1)}, s32[128,8]{0,1:T(8,128)}, u32[]{:S(2)}) copy-start(s32[128,8]{0,1:T(8,128)} %param.17) | copy-start | bytes 12292
  324.2 47.5 %all-to-all-start.2 = ((bf16[64,176,128]{2,1,0:T(8,128)(2,1)}), bf16[64,176,128]{2,1,0:T(8,128)(2,1)S(1)}, u32[]{:S(2)}, u32[]{:S(2)}) async-start(bf16[64,176,128]{2,1,0:T(8,128)(2,1)} %fusion.12), calls=%async_computation.2 | async-start | bytes 5767168 | tf_op jit(solution)/shard_map/all_to_all | solution.py:46
  378.4 2.0 copy-start.3
  380.4 3.7 copy-start.6
  384.1 1.1 copy-start.13
  385.1 5.4 %copy-start.4 = (bf16[128,7168]{1,0:T(8,128)(2,1)}, bf16[128,7168]{1,0:T(8,128)(2,1)S(1)}, u32[]{:S(2)}) copy-start(bf16[128,7168]{1,0:T(8,128)(2,1)S(1)} %add_convert_fusion) | copy-start | bytes 5505028
  391.2 2.5 collective-permute-start.11
  412.5 21.4 %copy-start.1 = (bf16[16,16384]{1,0:T(8,128)(2,1)S(1)}, bf16[16,16384]{1,0:T(8,128)(2,1)}, u32[]{:S(2)}) copy-start(bf16[16,16384]{1,0:T(8,128)(2,1)} %param.13) | copy-start | bytes 1572868
  427.2 4.6 %collective-permute-start.12 = (bf16[64,24,128]{2,1,0:T(8,128)(2,1)S(1)}, bf16[64,24,128]{2,1,0:T(8,128)(2,1)S(1)}, u32[]{:S(2)}, u32[]{:S(2)}) collective-permute-start(bf16[64,24,128]{2,1,0:T(8,128)(2,1)S(1)} %all_to_all.26), channel_id=1, source_target_pairs={{0,1},{1,0},{2,3},{3,2},{4,5},{5,4},{6,7},{7,6},{8,9},{9,8},{10,11... | collective-permute-start | bytes 1179656 | tf_op jit(solution)/shard_map/ppermute | solution.py:42
